TPU v7x, 256 devices: a whole 4x4x8 slice. The times are simulated.
256 devices in a mesh: grp: 4 (over y_hi, core), fsdp: 64 (over y_lo, x, z).
Axes of the slice: x: 4, y: 4 (y_hi: 2, y_lo: 2; y = y_hi * 2 + y_lo), z: 8, core: 2. Of those that a mesh axis runs over, the one named last changes fastest.
Arguments:
- traj_hidden: bfloat16 [262144, 4096], P(('grp', 'fsdp')), may hold values from -24 to 24
- traj_tokens: int32 [262144], P(('grp', 'fsdp')), may hold values from 0 to 511
- traj_action: int32 [262144], P(('grp', 'fsdp')), may hold values from 0 to 511
- traj_return: float32 [262144], P(('grp', 'fsdp')), may hold values from -6 to 6
- traj_episode: int32 [256, 1024], P(('grp', 'fsdp')), may hold values from 0 to 7, never falling along the last dimension, each value on 1 to 512 neighbouring positions
- roll_hidden: bfloat16 [16384, 4096], P(('grp', 'fsdp')), may hold values from -6 to 6
- roll_tokens: int32 [16384], P(('grp', 'fsdp')), may hold values from 0 to 511
- roll_action: int32 [16384], P(('grp', 'fsdp')), may hold values from 0 to 511
- station_table: bfloat16 [512, 4096], replicated, may hold values from -3 to 3
- norm_gain: float32 [4096], replicated, may hold values from 0.7 to 3.9
- head_weight: bfloat16 [4096, 512], P('fsdp'), may hold values from -6 to 6
Outputs:
- new_head: bfloat16 [4096, 512], P('fsdp')
- action_logp: float32 [16384], P(('grp', 'fsdp'))
- episode_logp: float32 [256], P(('grp', 'fsdp'))
Inputs may be any that keep to these rules, and one draw needn't show every extreme that they name: `traj_episode`: within each block of 1024 tokens the episode numbers never fall and every number 0 to 7 occurs.
All inputs are finite; a program needn't handle non-finite values.
Results may differ from a plain program's by a relative error of at most 0.0034.
Values may be sent and summed in bfloat16 or wider, within the bound.
A program may use at most 64 MiB of HBM per device.

v0:
```python
import jax
import jax.numpy as jnp
from jax import lax
from jax.sharding import PartitionSpec as P

ACTIONS = 512
STATIONS = 512
EPI_BLK = 8
STEPS = 64
step_length = 8.0


def station_rows(hidden, tokens, table, gain):
    lookup = (tokens[:, None] == jnp.arange(STATIONS, dtype=jnp.int32)[None, :]).astype(
        jnp.bfloat16
    )
    embedded = jnp.dot(lookup, table, preferred_element_type=jnp.float32)
    mixed = hidden.astype(jnp.float32) + embedded
    power = jnp.mean(mixed * mixed, axis=-1, keepdims=True)
    return (mixed * lax.rsqrt(power + 1e-05) * gain).astype(jnp.bfloat16)


def add_columns(left, piece):
    return jnp.dot(left, piece, preferred_element_type=jnp.float32)


def picked_logp(logits, actions):
    top = jnp.max(logits, axis=-1, keepdims=True)
    total = jnp.log(jnp.sum(jnp.exp(logits - top), axis=-1)) + top[:, 0]
    chosen = (actions[:, None] == jnp.arange(ACTIONS, dtype=jnp.int32)[None, :]).astype(jnp.float32)
    return jnp.sum(logits * chosen, axis=-1) - total


def episode_advantage(returns, episode):
    member = (episode[:, None] == jnp.arange(EPI_BLK, dtype=jnp.int32)[None, :]).astype(jnp.float32)
    sums = jnp.dot(member.T, returns, precision=lax.Precision.HIGHEST)
    counts = jnp.sum(member, axis=0)
    baseline = jnp.dot(member, sums / counts, precision=lax.Precision.HIGHEST)
    return returns - baseline


def outer_rows(left, right):
    return lax.dot_general(
        left, right, (((0,), (0,)), ((), ())), preferred_element_type=jnp.float32
    )


def local(
    traj_hidden,
    traj_tokens,
    traj_action,
    traj_return,
    traj_episode,
    roll_hidden,
    roll_tokens,
    roll_action,
    station_table,
    norm_gain,
    head_weight,
):
    features = station_rows(traj_hidden, traj_tokens, station_table, norm_gain)
    rollout = station_rows(roll_hidden, roll_tokens, station_table, norm_gain)
    advantage = episode_advantage(traj_return, traj_episode[0])
    logits = add_columns(features, lax.all_gather(head_weight, "fsdp", axis=0, tiled=True))
    top = jnp.max(logits, axis=-1, keepdims=True)
    expo = jnp.exp(logits - top)
    probs = expo / jnp.sum(expo, axis=-1, keepdims=True)
    chosen = (traj_action[:, None] == jnp.arange(ACTIONS, dtype=jnp.int32)[None, :]).astype(
        jnp.float32
    )
    scores = (advantage[:, None] * (probs - chosen)).astype(jnp.bfloat16)
    gathered, all_scores = (features, scores)
    grad_shard = lax.psum_scatter(
        outer_rows(gathered, all_scores), "fsdp", scatter_dimension=0, tiled=True
    )
    grad_shard = lax.psum(grad_shard, "grp")
    squares = lax.psum(jnp.sum(grad_shard * grad_shard), "fsdp")
    gnorm = jnp.sqrt(squares + 1e-06)
    new_head = (head_weight.astype(jnp.float32) - step_length * grad_shard / gnorm).astype(
        jnp.bfloat16
    )
    roll_logits = add_columns(rollout, lax.all_gather(new_head, "fsdp", axis=0, tiled=True))
    action_logp = picked_logp(roll_logits, roll_action)
    episode_logp = jnp.sum(action_logp.reshape(-1, STEPS), axis=1)
    return (new_head, action_logp, episode_logp)


def solution(mesh):
    placed = (
        P(("grp", "fsdp"), None),
        P(("grp", "fsdp")),
        P(("grp", "fsdp")),
        P(("grp", "fsdp")),
        P(("grp", "fsdp"), None),
        P(("grp", "fsdp"), None),
        P(("grp", "fsdp")),
        P(("grp", "fsdp")),
        P(),
        P(),
        P("fsdp", None),
    )
    return jax.shard_map(
        local,
        mesh=mesh,
        in_specs=placed,
        out_specs=(P("fsdp", None), P(("grp", "fsdp")), P(("grp", "fsdp"))),
        check_vma=False,
    )
```

profile of v0, /device:TPU:16, one launch (start us, length us, event | category | flops | bytes accessed | tf_op | source)
XLA Modules:
  0.0 1174.0 jit_solution(12649572377093902791)
XLA Ops:
  7.2 0.0 all-gather.3.cloned.1.call-start
  7.2 0.7 all-gather.3.cloned.1.call-update
  7.9 0.0 reduce-scatter.2.cloned.1.call-start
  7.9 0.8 convert_reduce_fusion
  8.8 0.8 fusion.3
  9.6 0.9 fusion.14
  10.4 0.7 sub.30
  11.1 0.0 copy-start.3
  11.1 8.8 multiply_reduce_fusion
  19.9 0.0 copy-done.3
  20.0 8.9 multiply_convert_fusion
  28.8 0.0 copy-start.6
  28.8 287.5 %all-gather.3.cloned.1.call-done = bf16[4096,512]{1,0:T(8,128)(2,1)} async-done(((bf16[64,512]{1,0:T(8,128)(2,1)}), bf16[4096,512]{1,0:T(8,128)(2,1)}) %all-gather.3.cloned.1.call-update) | async-done | bytes 4194320 | tf_op jit(solution)/shard_map/all_gather | solution.py:64
  316.3 0.0 copy-start
  316.3 8.4 fusion.18
  324.7 0.3 fusion.1
  325.1 0.0 copy-done.6
  325.1 0.0 copy-done
  325.1 7.7 fusion.4
  332.7 0.0 copy-start.2
  332.8 0.0 copy-start.1
  332.8 0.0 copy-start.4
  332.8 0.0 reduce-scatter.2.cloned.1.call-update
  332.8 0.0 all-reduce.2.cloned.1.call-start
  332.8 329.6 %reduce-scatter.2.cloned.1.call-done = f32[64,512]{1,0:T(8,128)} async-done(((f32[4096,512]{1,0:T(8,128)}), f32[64,512]{1,0:T(8,128)}) %reduce-scatter.2.cloned.1.call-update) | async-done | bytes 131088 | tf_op jit(solution)/shard_map/reduce_scatter | solution.py:73
  662.4 0.0 all-reduce.2.cloned.1.call-update
  662.5 0.0 all-gather.5.cloned.1.call-start
  662.5 39.2 %all-reduce.2.cloned.1.call-done = f32[64,512]{1,0:T(8,128)} async-done(((f32[64,512]{1,0:T(8,128)}), f32[64,512]{1,0:T(8,128)}) %all-reduce.2.cloned.1.call-update) | async-done | bytes 131088 | tf_op jit(solution)/shard_map/psum | solution.py:76
  701.7 1.5 multiply_reduce_fusion.2
  703.3 159.9 %psum.15 = f32[]{:T(128)} all-reduce(f32[]{:T(128)} %multiply_reduce_fusion.2), channel_id=1, replica_groups=mesh['grp'=4,'fsdp'=64] {'fsdp'}, use_global_device_ids=true, to_apply=%region_7.0 | all-reduce | flops 1 | bytes 8 | tf_op jit(solution)/shard_map/psum | solution.py:77
  863.8 0.0 copy-done.2
  863.8 1.6 subtract_convert_fusion
  865.4 0.0 all-gather.5.cloned.1.call-update
  865.4 0.0 copy-done.1
  865.4 0.0 copy-done.4
  865.4 0.0 copy-start.5
  865.4 3.2 multiply_reduce_fusion.1
  868.7 294.3 %all-gather.5.cloned.1.call-done = bf16[4096,512]{1,0:T(8,128)(2,1)} async-done(((bf16[64,512]{1,0:T(8,128)(2,1)}), bf16[4096,512]{1,0:T(8,128)(2,1)}) %all-gather.5.cloned.1.call-update) | async-done | bytes 4194320 | tf_op jit(solution)/shard_map/all_gather | solution.py:82
  1163.0 3.2 fusion.19
  1166.2 0.0 copy-done.5
  1166.2 0.2 exponential_reduce_fusion
  1166.4 1.1 fusion.17
  (2 shorter events, 0.0 us)
Async XLA Ops:
  7.2 309.2 %all-gather.3.cloned.1.call-start = ((), (), s32[]{:S(2)}) async-start(), calls=%async_computation.1 | async-start | bytes 4259840 | tf_op jit(solution)/shard_map/all_gather | solution.py:64
  7.9 654.5 %reduce-scatter.2.cloned.1.call-start = ((), (), s32[]{:S(2)}) async-start(), calls=%async_computation.2 | async-start | bytes 8519680 | tf_op jit(solution)/shard_map/reduce_scatter | solution.py:73
  11.1 8.8 copy-start.3
  28.8 296.3 %copy-start.6 = (s32[1024]{0:T(1024)S(1)}, s32[1024]{0:T(1024)}, u32[]{:S(2)}) copy-start(s32[1024]{0:T(1024)} %param.13) | copy-start | bytes 12292
  316.3 8.8 copy-start
  332.7 531.1 %copy-start.2 = (bf16[64,512]{1,0:T(8,128)(2,1)S(1)}, bf16[64,512]{1,0:T(8,128)(2,1)}, u32[]{:S(2)}) copy-start(bf16[64,512]{1,0:T(8,128)(2,1)} %param.21) | copy-start | bytes 196612
  332.8 532.7 %copy-start.1 = (bf16[64,4096]{1,0:T(8,128)(2,1)S(1)}, bf16[64,4096]{1,0:T(8,128)(2,1)}, u32[]{:S(2)}) copy-start(bf16[64,4096]{1,0:T(8,128)(2,1)} %param.16) | copy-start | bytes 1572868
  332.8 532.7 %copy-start.4 = (s32[64]{0:T(128)S(1)}, s32[64]{0:T(128)}, u32[]{:S(2)}) copy-start(s32[64]{0:T(128)} %param.17) | copy-start | bytes 772
  332.8 369.0 %all-reduce.2.cloned.1.call-start = ((), (), s32[]{:S(2)}) async-start(), calls=%async_computation.3 | async-start | bytes 262144 | tf_op jit(solution)/shard_map/psum | solution.py:76
  662.5 500.5 %all-gather.5.cloned.1.call-start = ((), (), s32[]{:S(2)}) async-start(), calls=%async_computation.4 | async-start | bytes 4259840 | tf_op jit(solution)/shard_map/all_gather | solution.py:82
  865.4 300.7 %copy-start.5 = (s32[64]{0:T(128)S(1)}, s32[64]{0:T(128)}, u32[]{:S(2)}) copy-start(s32[64]{0:T(128)} %param.18) | copy-start | bytes 772
Sparse Core Ops, SparseCore 0:
  9.8 306.4 all-gather.2
  332.9 329.4 reduce-scatter.1
  665.1 36.6 all-reduce.1
  865.5 297.4 all-gather.4
where the time goes:
time: 1170 us
  waiting for transfers between devices  951 us (81%)
  blocking collectives  160 us (14%)
  matrix products  32.9 us (3%)
  other arithmetic  15.1 us (1%)
  between operations  14.6 us (1%)
    reduce_scatter x1, waiting for transfers between devices, local(): lax.psum_scatter(outer_rows(gathered, all_scores), 'fsdp', scatter_dimens...  330 us
    all_gather x1, waiting for transfers between devices, local(): lax.all_gather(new_head, 'fsdp', axis=0, tiled=True)  294 us
    all_gather x1, waiting for transfers between devices, local(): lax.all_gather(head_weight, 'fsdp', axis=0, tiled=True)  288 us
    psum x1, blocking collectives, local(): squares = lax.psum(jnp.sum(grad_shard * grad_shard), 'fsdp')  160 us
    psum x1, waiting for transfers between devices, local(): grad_shard = lax.psum(grad_shard, 'grp')  39.2 us
  transfers between devices with their start and end apart: 4, of which 4 were waited for; matrix products, arithmetic and copies ran while one was open for 2% of the time, Pallas kernels for 0%

commit v1 on v0

--- a/solution.py
+++ b/solution.py
@@ -73,7 +73,7 @@
     grad_shard = lax.psum_scatter(
         outer_rows(gathered, all_scores), "fsdp", scatter_dimension=0, tiled=True
     )
-    grad_shard = lax.psum(grad_shard, "grp")
+    grad_shard = jnp.sum(lax.all_gather(grad_shard, "grp"), axis=0)
     squares = lax.psum(jnp.sum(grad_shard * grad_shard), "fsdp")
     gnorm = jnp.sqrt(squares + 1e-06)
     new_head = (head_weight.astype(jnp.float32) - step_length * grad_shard / gnorm).astype(

time: 1170 us -> 1140 us (0.974)
  waiting for transfers between devices: 951 us -> 912 us
    psum x1 -> x0, waiting for transfers between devices: 39.2 us -> none  [local(): grad_shard = lax.psum(grad_shard, 'grp')]
  transfers between devices with their start and end apart: 4 -> 3, of which waited for: 4 -> 3; matrix products, arithmetic and copies ran while one was open for 2% -> 2% of each run, Pallas kernels for 0% -> 0%
where the time goes in v1:
time: 1140 us
  waiting for transfers between devices  912 us (80%)
  blocking collectives  163 us (14%)
  matrix products  32.9 us (3%)
  between operations  14.5 us (1%)
  other arithmetic  13.4 us (1%)
    reduce_scatter x1, waiting for transfers between devices, local(): lax.psum_scatter(outer_rows(gathered, all_scores), 'fsdp', scatter_dimens...  330 us
    all_gather x1, waiting for transfers between devices, local(): lax.all_gather(new_head, 'fsdp', axis=0, tiled=True)  294 us
    all_gather x1, waiting for transfers between devices, local(): lax.all_gather(head_weight, 'fsdp', axis=0, tiled=True)  288 us
    psum x1, blocking collectives, local(): squares = lax.psum(jnp.sum(grad_shard * grad_shard), 'fsdp')  155 us
  transfers between devices with their start and end apart: 3, of which 3 were waited for; matrix products, arithmetic and copies ran while one was open for 2% of the time, Pallas kernels for 0%

profile of v1, /device:TPU:16, one launch (start us, length us, event | category | flops | bytes accessed | tf_op | source)
XLA Modules:
  0.0 1135.9 jit_solution(4385023929642320360)
XLA Ops:
  7.2 0.0 all-gather.4.cloned.1.call-start
  7.2 0.7 all-gather.4.cloned.1.call-update
  7.9 0.0 reduce-scatter.2.cloned.1.call-start
  7.9 0.8 convert_reduce_fusion
  8.8 0.8 fusion.3
  9.6 0.9 fusion.14
  10.4 0.7 sub.30
  11.1 0.0 copy-start.3
  11.1 8.8 multiply_reduce_fusion
  19.9 0.0 copy-done.3
  20.0 8.9 multiply_convert_fusion
  28.8 0.0 copy-start.6
  28.8 287.5 %all-gather.4.cloned.1.call-done = bf16[4096,512]{1,0:T(8,128)(2,1)} async-done(((bf16[64,512]{1,0:T(8,128)(2,1)}), bf16[4096,512]{1,0:T(8,128)(2,1)}) %all-gather.4.cloned.1.call-update) | async-done | bytes 4194320 | tf_op jit(solution)/shard_map/all_gather | solution.py:64
  316.3 0.0 copy-start
  316.3 8.4 fusion.18
  324.7 0.3 fusion.1
  325.1 0.0 copy-done.6
  325.1 0.0 copy-done
  325.1 7.7 fusion.4
  332.7 0.0 copy-start.2
  332.8 0.0 copy-start.1
  332.8 0.0 copy-start.4
  332.8 0.0 reduce-scatter.2.cloned.1.call-update
  332.8 0.0 all-gather.6.cloned.1.call-start
  332.8 329.6 %reduce-scatter.2.cloned.1.call-done = f32[64,512]{1,0:T(8,128)} async-done(((f32[4096,512]{1,0:T(8,128)}), f32[64,512]{1,0:T(8,128)}) %reduce-scatter.2.cloned.1.call-update) | async-done | bytes 131088 | tf_op jit(solution)/shard_map/reduce_scatter | solution.py:73
  662.4 8.2 all-gather
  670.7 0.6 multiply_reduce_fusion.2
  671.3 154.5 %psum.7 = f32[]{:T(128)} all-reduce(f32[]{:T(128)} %multiply_reduce_fusion.2), channel_id=1, replica_groups=mesh['grp'=4,'fsdp'=64] {'fsdp'}, use_global_device_ids=true, to_apply=%region_7.0 | all-reduce | flops 1 | bytes 8 | tf_op jit(solution)/shard_map/psum | solution.py:77
  826.5 0.0 copy-done.2
  826.5 0.7 subtract_convert_fusion
  827.2 0.0 all-gather.6.cloned.1.call-update
  827.2 0.0 copy-done.1
  827.2 0.0 copy-done.4
  827.2 0.0 copy-start.5
  827.3 3.2 multiply_reduce_fusion.1
  830.5 294.3 %all-gather.6.cloned.1.call-done = bf16[4096,512]{1,0:T(8,128)(2,1)} async-done(((bf16[64,512]{1,0:T(8,128)(2,1)}), bf16[4096,512]{1,0:T(8,128)(2,1)}) %all-gather.6.cloned.1.call-update) | async-done | bytes 4194320 | tf_op jit(solution)/shard_map/all_gather | solution.py:82
  1124.8 3.2 fusion.19
  1128.0 0.0 copy-done.5
  1128.0 0.2 exponential_reduce_fusion
  1128.2 1.1 fusion.17
  (3 shorter events, 0.0 us)
Async XLA Ops:
  7.2 309.2 %all-gather.4.cloned.1.call-start = ((), (), s32[]{:S(2)}) async-start(), calls=%async_computation.1 | async-start | bytes 4259840 | tf_op jit(solution)/shard_map/all_gather | solution.py:64
  7.9 654.5 %reduce-scatter.2.cloned.1.call-start = ((), (), s32[]{:S(2)}) async-start(), calls=%async_computation.2 | async-start | bytes 8519680 | tf_op jit(solution)/shard_map/reduce_scatter | solution.py:73
  11.1 8.8 copy-start.3
  28.8 296.3 %copy-start.6 = (s32[1024]{0:T(1024)S(1)}, s32[1024]{0:T(1024)}, u32[]{:S(2)}) copy-start(s32[1024]{0:T(1024)} %param.13) | copy-start | bytes 12292
  316.3 8.8 copy-start
  332.7 493.8 %copy-start.2 = (bf16[64,512]{1,0:T(8,128)(2,1)S(1)}, bf16[64,512]{1,0:T(8,128)(2,1)}, u32[]{:S(2)}) copy-start(bf16[64,512]{1,0:T(8,128)(2,1)} %param.21) | copy-start | bytes 196612
  332.8 494.5 %copy-start.1 = (bf16[64,4096]{1,0:T(8,128)(2,1)S(1)}, bf16[64,4096]{1,0:T(8,128)(2,1)}, u32[]{:S(2)}) copy-start(bf16[64,4096]{1,0:T(8,128)(2,1)} %param.16) | copy-start | bytes 1572868
  332.8 494.5 %copy-start.4 = (s32[64]{0:T(128)S(1)}, s32[64]{0:T(128)}, u32[]{:S(2)}) copy-start(s32[64]{0:T(128)} %param.17) | copy-start | bytes 772
  332.8 792.0 %all-gather.6.cloned.1.call-start = ((), (), s32[]{:S(2)}) async-start(), calls=%async_computation.3 | async-start | bytes 4259840 | tf_op jit(solution)/shard_map/all_gather | solution.py:82
  827.2 300.7 %copy-start.5 = (s32[64]{0:T(128)S(1)}, s32[64]{0:T(128)}, u32[]{:S(2)}) copy-start(s32[64]{0:T(128)} %param.18) | copy-start | bytes 772
Sparse Core Ops, SparseCore 0:
  9.8 306.4 all-gather.3
  332.9 329.4 reduce-scatter.1
  827.3 297.4 all-gather.5

commit v2 on v0

--- a/solution.py
+++ b/solution.py
@@ -79,7 +79,12 @@
     new_head = (head_weight.astype(jnp.float32) - step_length * grad_shard / gnorm).astype(
         jnp.bfloat16
     )
-    roll_logits = add_columns(rollout, lax.all_gather(new_head, "fsdp", axis=0, tiled=True))
+    roll_logits = add_columns(
+        rollout,
+        jnp.concatenate(
+            lax.all_to_all(jnp.stack([new_head] * lax.axis_size("fsdp")), "fsdp", 0, 0), axis=0
+        ),
+    )
     action_logp = picked_logp(roll_logits, roll_action)
     episode_logp = jnp.sum(action_logp.reshape(-1, STEPS), axis=1)
     return (new_head, action_logp, episode_logp)

time: 1170 us -> 955 us (0.82)
  waiting for transfers between devices: 951 us -> 721 us
    all_gather x1 -> x0, waiting for transfers between devices: 294 us -> none  [local(): lax.all_gather(new_head, 'fsdp', axis=0, tiled=True)]
    all_to_all x0 -> x1, waiting for transfers between devices: none -> 63.7 us  [local(): lax.all_to_all(jnp.stack([new_head] * lax.axis_size('fsdp')), 'fsdp', 0, 0)]
  transfers between devices with their start and end apart: 4 -> 4, of which waited for: 4 -> 4; matrix products, arithmetic and copies ran while one was open for 2% -> 3% of each run, Pallas kernels for 0% -> 0%
where the time goes in v2:
time: 955 us; the launch traced here: 952 us
  waiting for transfers between devices  721 us (75%)
  blocking collectives  161 us (17%)
  matrix products  32.9 us (3%)
  between operations  14.6 us (2%)
  other arithmetic  14.5 us (2%)
    reduce_scatter x1, waiting for transfers between devices, local(): lax.psum_scatter(outer_rows(gathered, all_scores), 'fsdp', scatter_dimens...  330 us
    all_gather x1, waiting for transfers between devices, local(): lax.all_gather(head_weight, 'fsdp', axis=0, tiled=True)  288 us
    psum x1, blocking collectives, local(): squares = lax.psum(jnp.sum(grad_shard * grad_shard), 'fsdp')  161 us
    all_to_all x1, waiting for transfers between devices, local(): lax.all_to_all(jnp.stack([new_head] * lax.axis_size('fsdp')), 'fsdp', 0, 0)  63.7 us
    psum x1, waiting for transfers between devices, local(): grad_shard = lax.psum(grad_shard, 'grp')  39.4 us
  transfers between devices with their start and end apart: 4, of which 4 were waited for; matrix products, arithmetic and copies ran while one was open for 3% of the time, Pallas kernels for 0%

profile of v2, /device:TPU:16, one launch (start us, length us, event | category | flops | bytes accessed | tf_op | source)
XLA Modules:
  0.0 952.3 jit_solution(6792862771197155516)
XLA Ops:
  7.2 0.0 all-gather.2.cloned.1.call-start
  7.2 0.7 all-gather.2.cloned.1.call-update
  7.9 0.0 reduce-scatter.2.cloned.1.call-start
  7.9 0.8 convert_reduce_fusion
  8.8 0.8 fusion.3
  9.6 0.9 fusion.14
  10.4 0.7 sub.30
  11.1 0.0 copy-start.4
  11.1 8.8 multiply_reduce_fusion
  19.9 0.0 copy-done.4
  20.0 8.9 multiply_convert_fusion
  28.8 0.0 copy-start.7
  28.8 287.5 %all-gather.2.cloned.1.call-done = bf16[4096,512]{1,0:T(8,128)(2,1)} async-done(((bf16[64,512]{1,0:T(8,128)(2,1)}), bf16[4096,512]{1,0:T(8,128)(2,1)}) %all-gather.2.cloned.1.call-update) | async-done | bytes 4194320 | tf_op jit(solution)/shard_map/all_gather | solution.py:64
  316.3 0.0 copy-start
  316.3 8.4 fusion.18
  324.7 0.3 fusion.1
  325.1 0.0 copy-done.7
  325.1 0.0 copy-done
  325.1 7.7 fusion.4
  332.7 0.0 copy-start.3
  332.8 0.0 reduce-scatter.2.cloned.1.call-update
  332.8 0.0 all-reduce.2.cloned.1.call-start
  332.8 329.6 %reduce-scatter.2.cloned.1.call-done = f32[64,512]{1,0:T(8,128)} async-done(((f32[4096,512]{1,0:T(8,128)}), f32[64,512]{1,0:T(8,128)}) %reduce-scatter.2.cloned.1.call-update) | async-done | bytes 131088 | tf_op jit(solution)/shard_map/reduce_scatter | solution.py:73
  662.4 0.0 all-reduce.2.cloned.1.call-update
  662.5 39.4 %all-reduce.2.cloned.1.call-done = f32[64,512]{1,0:T(8,128)} async-done(((f32[64,512]{1,0:T(8,128)}), f32[64,512]{1,0:T(8,128)}) %all-reduce.2.cloned.1.call-update) | async-done | bytes 131088 | tf_op jit(solution)/shard_map/psum | solution.py:76
  701.8 1.5 multiply_reduce_fusion.2
  703.4 161.0 %psum.15 = f32[]{:T(128)} all-reduce(f32[]{:T(128)} %multiply_reduce_fusion.2), channel_id=1, replica_groups=mesh['grp'=4,'fsdp'=64] {'fsdp'}, use_global_device_ids=true, to_apply=%region_7.0 | all-reduce | flops 1 | bytes 8 | tf_op jit(solution)/shard_map/psum | solution.py:77
  865.1 0.0 copy-done.3
  865.1 0.9 subtract_convert_fusion
  866.0 0.0 copy-start.2
  866.0 2.5 stack.2
  868.5 0.0 copy-start.1
  868.5 0.0 copy-start.5
  868.5 0.0 copy-done.2
  868.5 5.8 all-to-all-start
  874.3 0.0 copy-done.1
  874.3 0.0 copy-done.5
  874.3 0.0 copy-start.6
  874.3 3.2 multiply_reduce_fusion.1
  877.6 63.7 %all-to-all-done = bf16[64,64,512]{2,1,0:T(8,128)(2,1)} async-done(((bf16[64,64,512]{2,1,0:T(8,128)(2,1)}), bf16[64,64,512]{2,1,0:T(8,128)(2,1)}, u32[]{:S(2)}, u32[]{:S(2)}) %all-to-all-start) | async-done | bytes 4194336 | tf_op jit(solution)/shard_map/all_to_all | solution.py:85
  941.2 3.2 fusion.19
  944.4 0.0 copy-done.6
  944.4 0.2 exponential_reduce_fusion
  944.6 1.1 fusion.17
  (2 shorter events, 0.0 us)
Async XLA Ops:
  7.2 309.2 %all-gather.2.cloned.1.call-start = ((), (), s32[]{:S(2)}) async-start(), calls=%async_computation.2 | async-start | bytes 4259840 | tf_op jit(solution)/shard_map/all_gather | solution.py:64
  7.9 654.5 %reduce-scatter.2.cloned.1.call-start = ((), (), s32[]{:S(2)}) async-start(), calls=%async_computation.3 | async-start | bytes 8519680 | tf_op jit(solution)/shard_map/reduce_scatter | solution.py:73
  11.1 8.8 copy-start.4
  28.8 296.3 %copy-start.7 = (s32[1024]{0:T(1024)S(1)}, s32[1024]{0:T(1024)}, u32[]{:S(2)}) copy-start(s32[1024]{0:T(1024)} %param.13) | copy-start | bytes 12292
  316.3 8.8 copy-start
  332.7 532.3 %copy-start.3 = (bf16[64,512]{1,0:T(8,128)(2,1)S(1)}, bf16[64,512]{1,0:T(8,128)(2,1)}, u32[]{:S(2)}) copy-start(bf16[64,512]{1,0:T(8,128)(2,1)} %param.21) | copy-start | bytes 196612
  332.8 369.1 %all-reduce.2.cloned.1.call-start = ((), (), s32[]{:S(2)}) async-start(), calls=%async_computation.4 | async-start | bytes 262144 | tf_op jit(solution)/shard_map/psum | solution.py:76
  866.0 2.5 copy-start.2
  868.5 5.8 copy-start.1
  868.5 5.8 copy-start.5
  868.5 72.7 %all-to-all-start = ((bf16[64,64,512]{2,1,0:T(8,128)(2,1)}), bf16[64,64,512]{2,1,0:T(8,128)(2,1)}, u32[]{:S(2)}, u32[]{:S(2)}) async-start(bf16[64,64,512]{2,1,0:T(8,128)(2,1)} %stack.2), calls=%async_computation.1 | async-start | bytes 8388608 | tf_op jit(solution)/shard_map/all_to_all | solution.py:85
  874.3 70.1 %copy-start.6 = (s32[64]{0:T(128)S(1)}, s32[64]{0:T(128)}, u32[]{:S(2)}) copy-start(s32[64]{0:T(128)} %param.18) | copy-start | bytes 772
Sparse Core Ops, SparseCore 0:
  9.8 306.4 all-gather.1
  332.9 329.4 reduce-scatter.1
  665.1 36.7 all-reduce.1
